TPU v7x, 256 devices: a whole 4x4x8 slice. The times are simulated.
256 devices in a mesh: tile: 64 (over y, z, core), sec: 4 (over x).
Axes of the slice: x: 4, y: 4, z: 8, core: 2. Of those that a mesh axis runs over, the one named last changes fastest.
Arguments:
- voltage: float32 [8192, 512], P('tile', 'sec'), may hold values from -6 to 6
- conductance: float32 [8192, 512], P('tile', 'sec'), may hold values from 0.2 to 2
- reversal: float32 [8192, 512], P('tile', 'sec'), may hold values from -1 to 1
- drive: bfloat16 [8, 8192, 512], P(None, 'tile', 'sec'), may hold values from -6 to 6
- inv_cable: float32 [128, 128], replicated, may hold values from -1 to 1
- owner_map: int32 [8192], P('tile'), may hold values from 0 to 63, as said below
- peer_counts: int32 [64, 64], P('tile'), may hold values from 0 to 4, as said below
- pattern: int32 [4, 8192, 2], P('sec', 'tile'), may hold values from 0 to 31, all different within a row
- transfer: bfloat16 [4, 8192, 2, 128, 128], P('sec', 'tile'), may hold values from -0.01171875 to 0.01171875
Outputs:
- final_voltage: float32 [8192, 512], P('tile', 'sec')
- probe: float32 [8, 4096], P(None, ('tile', 'sec'))
Inputs may be any that keep to these rules, and one draw needn't show every extreme that they name: `owner_map`: every depth tile owns exactly 128 cells; the cells c with c // 128 = u include at most 4 cells of one owner, and exactly 4 of some owner. peer_counts[d, u] is the number of cells c with c // 128 = u and owner_map[c] = d. `pattern`: the 2 contact tiles of one slot and section differ.
All inputs are finite; a program needn't handle non-finite values.
Results may differ from a plain program's by a relative error of at most 0.0029.
Values may be sent and summed in bfloat16 or wider, within the bound.
A program may use at most 64 MiB of HBM per device.

v0:
```python
import jax
import jax.numpy as jnp
from jax import lax
from jax.sharding import PartitionSpec as P

CONTACTS = 4096
TIME_STEP = 0.25
AXIAL = 2.0


def padded_2(block, sides, width):
    for axis, dim in sides:
        count = lax.axis_size(axis)
        forward = [(i, i + 1) for i in range(count - 1)]
        backward = [(target, source) for source, target in forward]
        low = lax.ppermute(
            lax.slice_in_dim(block, block.shape[dim] - width, None, axis=dim), axis, forward
        )
        high = lax.ppermute(lax.slice_in_dim(block, 0, width, axis=dim), axis, backward)
        block = jnp.concatenate([low, block, high], axis=dim)
    return block


def cable_update(voltage_now, conductance, reversal, drive_now, inv_cable):
    padded = padded_2(voltage_now.astype(jnp.bfloat16), (("sec", 1),), 1).astype(voltage_now.dtype)
    columns = jnp.arange(voltage_now.shape[1], dtype=jnp.int32)
    first_col = (columns == 0).astype(jnp.float32)
    last_col = (columns == voltage_now.shape[1] - 1).astype(jnp.float32)
    boundary = first_col * (padded[:, :-2] - voltage_now) + last_col * (padded[:, 2:] - voltage_now)
    driven = drive_now.astype(jnp.float32)
    right_side = voltage_now * (1.0 - TIME_STEP * conductance) + TIME_STEP * (
        conductance * reversal + driven + AXIAL * boundary
    )
    voltage_next = jnp.einsum("ci,ji->cj", right_side, inv_cable, precision=lax.Precision.HIGHEST)
    current = (conductance * (voltage_next - reversal) - driven).astype(jnp.bfloat16)
    return (voltage_next, current)


def on_device(
    voltage, conductance, reversal, drive, inv_cable, owner_map, peer_counts, pattern, transfer
):
    cell_count = voltage.shape[0]
    seg_width = voltage.shape[1]
    step_count = drive.shape[0]
    tile_count = lax.axis_size("tile")
    section_count = lax.axis_size("sec")
    capacity = 2 * cell_count // tile_count
    owners = jnp.arange(tile_count, dtype=jnp.int32)
    member = (owner_map[:, None] == owners[None, :]).astype(jnp.int32)
    rank_within = jnp.sum(jnp.cumsum(member, axis=0) * member, axis=1) - 1
    placed = owner_map * capacity + rank_within
    source_row = (
        jnp.full((tile_count * capacity,), cell_count, jnp.int32)
        .at[placed]
        .set(jnp.arange(cell_count, dtype=jnp.int32))
    )
    blank_row = jnp.zeros((1, seg_width), jnp.bfloat16)

    def advance_send(voltage_now, drive_now):
        voltage_next, current = cable_update(
            voltage_now, conductance, reversal, drive_now, inv_cable
        )
        outgoing = jnp.take(jnp.concatenate([current, blank_row], axis=0), source_row, axis=0)
        outgoing = outgoing.reshape(tile_count, capacity, seg_width)
        arrived = lax.all_to_all(outgoing, "tile", split_axis=0, concat_axis=0, tiled=True)
        return (voltage_next, arrived)

    final_voltage, arrived = lax.scan(advance_send, voltage, drive)
    received = arrived.reshape(step_count, tile_count * capacity, seg_width)
    counts = peer_counts[0]
    end_rows = jnp.cumsum(counts)
    starts = end_rows - counts
    slot_ids = jnp.arange(cell_count, dtype=jnp.int32)
    source = jnp.sum((end_rows[None, :] <= slot_ids[:, None]).astype(jnp.int32), axis=1)
    offset = jnp.sum(jnp.where(source[:, None] == owners[None, :], starts[None, :], 0), axis=1)
    gather_rows = source * capacity + slot_ids - offset
    ordered = jnp.take(received, gather_rows, axis=1)
    weights = transfer[0]
    layout = pattern[0]
    contact_width = weights.shape[3]
    tile_total = CONTACTS // contact_width
    tile_sums = jnp.einsum("tsi,skic->tskc", ordered, weights, preferred_element_type=jnp.float32)
    select = (layout[:, :, None] == jnp.arange(tile_total, dtype=jnp.int32)[None, None, :]).astype(
        jnp.float32
    )
    partial_sum = jnp.einsum("tskc,skq->tqc", tile_sums, select, precision=lax.Precision.HIGHEST)
    partial_sum = partial_sum.reshape(step_count, tile_total * contact_width)
    summed = lax.psum(partial_sum, ("tile", "sec"))
    share_width = summed.shape[1] // (tile_count * section_count)
    position = lax.axis_index("tile") * section_count + lax.axis_index("sec")
    probe_share = lax.dynamic_slice_in_dim(summed, position * share_width, share_width, 1)
    return (final_voltage, probe_share)


def solution(mesh):
    placed = (
        P("tile", "sec"),
        P("tile", "sec"),
        P("tile", "sec"),
        P(None, "tile", "sec"),
        P(),
        P("tile"),
        P("tile", None),
        P("sec", "tile", None),
        P("sec", "tile", None, None, None),
    )
    return jax.shard_map(
        on_device,
        mesh=mesh,
        in_specs=placed,
        out_specs=(P("tile", "sec"), P(None, ("tile", "sec"))),
        check_vma=False,
    )
```

profile of v0, /device:TPU:8, one launch (start us, length us, event | category | flops | bytes accessed | tf_op | source)
XLA Modules:
  0.0 478.0 jit_solution(9085325909894427495)
XLA Ops:
  14.3 208.3 %while.13 = (s32[]{:T(128)}, f32[128,128]{1,0:T(8,128)S(1)}, bf16[8,64,4,128]{3,2,1,0:T(4,128)(2,1)S(1)}, f32[128,128]{1,0:T(8,128)}, bf16[8,128,128]{2,1,0:T(8,...) while((s32[]{:T(128)}, f32[128,128]{1,0:T(8,128)S(1)}, ...), condition=%wide.region_4.5_spmd, body=%wide.region_3.4_spmd.sunk | while | flops 25629952 | bytes 1626603 | solution.py:68
  14.4 1.3 collective-permute-start
  15.7 4.5 collective-permute-start.1
  20.4 1.4 collective-permute-done.1
  21.9 1.3 fusion.52
  24.8 12.1 %all-to-all-start = ((bf16[64,4,128]{2,1,0:T(4,128)(2,1)}), bf16[64,4,128]{2,1,0:T(4,128)(2,1)S(1)}, u32[]{:S(2)}, u32[]{:S(2)}) async-start(bf16[64,4,128]{2,1,0:T(4,128)(2,1)} %broadcast_select_fusion.2), calls=%async_computation | async-start | bytes 131072 | tf_op jit(solution)/shard_map/while/body/eval_jaxpr/all_to_all | solution.py:65
  36.9 8.8 %all-to-all-done = bf16[64,4,128]{2,1,0:T(4,128)(2,1)S(1)} async-done(((bf16[64,4,128]{2,1,0:T(4,128)(2,1)}), bf16[64,4,128]{2,1,0:T(4,128)(2,1)S(1)}, u32[]{:S(2)}, u32[]{:S(2)}) %all-to-all-start) | async-done | bytes 65568 | tf_op jit(solution)/shard_map/while/body/eval_jaxpr/all_to_all | solution.py:65
  45.9 1.3 collective-permute-start
  47.2 4.9 %collective-permute-start.1 = (bf16[128,1]{1,0:T(8,128)(2,1)S(1)}, bf16[128,1]{1,0:T(8,128)(2,1)S(1)}, u32[]{:S(2)}, u32[]{:S(2)}) collective-permute-start(bf16[128,1]{1,0:T(8,128)(2,1)S(1)} %get-tuple-element.171), channel_id=1, source_target_pairs={{0,1},{1,2},{2,3},{4,5},{5,6},{6,7},{8,9},{9,10},{10,11},{12,13},{... | collective-permute-start | bytes 776 | tf_op jit(solution)/shard_map/while/body/eval_jaxpr/ppermute | solution.py:16
  52.2 1.4 collective-permute-done.1
  53.7 1.3 fusion.52
  56.7 5.5 %all-to-all-start = ((bf16[64,4,128]{2,1,0:T(4,128)(2,1)}), bf16[64,4,128]{2,1,0:T(4,128)(2,1)S(1)}, u32[]{:S(2)}, u32[]{:S(2)}) async-start(bf16[64,4,128]{2,1,0:T(4,128)(2,1)} %broadcast_select_fusion.2), calls=%async_computation | async-start | bytes 131072 | tf_op jit(solution)/shard_map/while/body/eval_jaxpr/all_to_all | solution.py:65
  62.2 8.8 %all-to-all-done = bf16[64,4,128]{2,1,0:T(4,128)(2,1)S(1)} async-done(((bf16[64,4,128]{2,1,0:T(4,128)(2,1)}), bf16[64,4,128]{2,1,0:T(4,128)(2,1)S(1)}, u32[]{:S(2)}, u32[]{:S(2)}) %all-to-all-start) | async-done | bytes 65568 | tf_op jit(solution)/shard_map/while/body/eval_jaxpr/all_to_all | solution.py:65
  71.2 1.3 collective-permute-start
  72.5 4.9 %collective-permute-start.1 = (bf16[128,1]{1,0:T(8,128)(2,1)S(1)}, bf16[128,1]{1,0:T(8,128)(2,1)S(1)}, u32[]{:S(2)}, u32[]{:S(2)}) collective-permute-start(bf16[128,1]{1,0:T(8,128)(2,1)S(1)} %get-tuple-element.171), channel_id=1, source_target_pairs={{0,1},{1,2},{2,3},{4,5},{5,6},{6,7},{8,9},{9,10},{10,11},{12,13},{... | collective-permute-start | bytes 776 | tf_op jit(solution)/shard_map/while/body/eval_jaxpr/ppermute | solution.py:16
  77.5 1.4 collective-permute-done.1
  79.0 1.3 fusion.52
  81.9 5.5 %all-to-all-start = ((bf16[64,4,128]{2,1,0:T(4,128)(2,1)}), bf16[64,4,128]{2,1,0:T(4,128)(2,1)S(1)}, u32[]{:S(2)}, u32[]{:S(2)}) async-start(bf16[64,4,128]{2,1,0:T(4,128)(2,1)} %broadcast_select_fusion.2), calls=%async_computation | async-start | bytes 131072 | tf_op jit(solution)/shard_map/while/body/eval_jaxpr/all_to_all | solution.py:65
  87.4 8.8 %all-to-all-done = bf16[64,4,128]{2,1,0:T(4,128)(2,1)S(1)} async-done(((bf16[64,4,128]{2,1,0:T(4,128)(2,1)}), bf16[64,4,128]{2,1,0:T(4,128)(2,1)S(1)}, u32[]{:S(2)}, u32[]{:S(2)}) %all-to-all-start) | async-done | bytes 65568 | tf_op jit(solution)/shard_map/while/body/eval_jaxpr/all_to_all | solution.py:65
  96.4 1.3 collective-permute-start
  97.7 4.9 %collective-permute-start.1 = (bf16[128,1]{1,0:T(8,128)(2,1)S(1)}, bf16[128,1]{1,0:T(8,128)(2,1)S(1)}, u32[]{:S(2)}, u32[]{:S(2)}) collective-permute-start(bf16[128,1]{1,0:T(8,128)(2,1)S(1)} %get-tuple-element.171), channel_id=1, source_target_pairs={{0,1},{1,2},{2,3},{4,5},{5,6},{6,7},{8,9},{9,10},{10,11},{12,13},{... | collective-permute-start | bytes 776 | tf_op jit(solution)/shard_map/while/body/eval_jaxpr/ppermute | solution.py:16
  102.8 1.4 collective-permute-done.1
  107.2 5.5 %all-to-all-start = ((bf16[64,4,128]{2,1,0:T(4,128)(2,1)}), bf16[64,4,128]{2,1,0:T(4,128)(2,1)S(1)}, u32[]{:S(2)}, u32[]{:S(2)}) async-start(bf16[64,4,128]{2,1,0:T(4,128)(2,1)} %broadcast_select_fusion.2), calls=%async_computation | async-start | bytes 131072 | tf_op jit(solution)/shard_map/while/body/eval_jaxpr/all_to_all | solution.py:65
  112.7 8.8 %all-to-all-done = bf16[64,4,128]{2,1,0:T(4,128)(2,1)S(1)} async-done(((bf16[64,4,128]{2,1,0:T(4,128)(2,1)}), bf16[64,4,128]{2,1,0:T(4,128)(2,1)S(1)}, u32[]{:S(2)}, u32[]{:S(2)}) %all-to-all-start) | async-done | bytes 65568 | tf_op jit(solution)/shard_map/while/body/eval_jaxpr/all_to_all | solution.py:65
  121.7 1.3 collective-permute-start
  123.0 4.9 %collective-permute-start.1 = (bf16[128,1]{1,0:T(8,128)(2,1)S(1)}, bf16[128,1]{1,0:T(8,128)(2,1)S(1)}, u32[]{:S(2)}, u32[]{:S(2)}) collective-permute-start(bf16[128,1]{1,0:T(8,128)(2,1)S(1)} %get-tuple-element.171), channel_id=1, source_target_pairs={{0,1},{1,2},{2,3},{4,5},{5,6},{6,7},{8,9},{9,10},{10,11},{12,13},{... | collective-permute-start | bytes 776 | tf_op jit(solution)/shard_map/while/body/eval_jaxpr/ppermute | solution.py:16
  128.0 1.4 collective-permute-done.1
  132.4 5.5 %all-to-all-start = ((bf16[64,4,128]{2,1,0:T(4,128)(2,1)}), bf16[64,4,128]{2,1,0:T(4,128)(2,1)S(1)}, u32[]{:S(2)}, u32[]{:S(2)}) async-start(bf16[64,4,128]{2,1,0:T(4,128)(2,1)} %broadcast_select_fusion.2), calls=%async_computation | async-start | bytes 131072 | tf_op jit(solution)/shard_map/while/body/eval_jaxpr/all_to_all | solution.py:65
  137.9 8.8 %all-to-all-done = bf16[64,4,128]{2,1,0:T(4,128)(2,1)S(1)} async-done(((bf16[64,4,128]{2,1,0:T(4,128)(2,1)}), bf16[64,4,128]{2,1,0:T(4,128)(2,1)S(1)}, u32[]{:S(2)}, u32[]{:S(2)}) %all-to-all-start) | async-done | bytes 65568 | tf_op jit(solution)/shard_map/while/body/eval_jaxpr/all_to_all | solution.py:65
  146.9 1.3 collective-permute-start
  148.2 4.9 %collective-permute-start.1 = (bf16[128,1]{1,0:T(8,128)(2,1)S(1)}, bf16[128,1]{1,0:T(8,128)(2,1)S(1)}, u32[]{:S(2)}, u32[]{:S(2)}) collective-permute-start(bf16[128,1]{1,0:T(8,128)(2,1)S(1)} %get-tuple-element.171), channel_id=1, source_target_pairs={{0,1},{1,2},{2,3},{4,5},{5,6},{6,7},{8,9},{9,10},{10,11},{12,13},{... | collective-permute-start | bytes 776 | tf_op jit(solution)/shard_map/while/body/eval_jaxpr/ppermute | solution.py:16
  153.3 1.4 collective-permute-done.1
  154.8 1.3 fusion.52
  157.7 5.5 %all-to-all-start = ((bf16[64,4,128]{2,1,0:T(4,128)(2,1)}), bf16[64,4,128]{2,1,0:T(4,128)(2,1)S(1)}, u32[]{:S(2)}, u32[]{:S(2)}) async-start(bf16[64,4,128]{2,1,0:T(4,128)(2,1)} %broadcast_select_fusion.2), calls=%async_computation | async-start | bytes 131072 | tf_op jit(solution)/shard_map/while/body/eval_jaxpr/all_to_all | solution.py:65
  163.2 8.8 %all-to-all-done = bf16[64,4,128]{2,1,0:T(4,128)(2,1)S(1)} async-done(((bf16[64,4,128]{2,1,0:T(4,128)(2,1)}), bf16[64,4,128]{2,1,0:T(4,128)(2,1)S(1)}, u32[]{:S(2)}, u32[]{:S(2)}) %all-to-all-start) | async-done | bytes 65568 | tf_op jit(solution)/shard_map/while/body/eval_jaxpr/all_to_all | solution.py:65
  172.2 1.3 collective-permute-start
  173.5 4.9 %collective-permute-start.1 = (bf16[128,1]{1,0:T(8,128)(2,1)S(1)}, bf16[128,1]{1,0:T(8,128)(2,1)S(1)}, u32[]{:S(2)}, u32[]{:S(2)}) collective-permute-start(bf16[128,1]{1,0:T(8,128)(2,1)S(1)} %get-tuple-element.171), channel_id=1, source_target_pairs={{0,1},{1,2},{2,3},{4,5},{5,6},{6,7},{8,9},{9,10},{10,11},{12,13},{... | collective-permute-start | bytes 776 | tf_op jit(solution)/shard_map/while/body/eval_jaxpr/ppermute | solution.py:16
  178.5 1.4 collective-permute-done.1
  182.9 5.5 %all-to-all-start = ((bf16[64,4,128]{2,1,0:T(4,128)(2,1)}), bf16[64,4,128]{2,1,0:T(4,128)(2,1)S(1)}, u32[]{:S(2)}, u32[]{:S(2)}) async-start(bf16[64,4,128]{2,1,0:T(4,128)(2,1)} %broadcast_select_fusion.2), calls=%async_computation | async-start | bytes 131072 | tf_op jit(solution)/shard_map/while/body/eval_jaxpr/all_to_all | solution.py:65
  188.5 8.8 %all-to-all-done = bf16[64,4,128]{2,1,0:T(4,128)(2,1)S(1)} async-done(((bf16[64,4,128]{2,1,0:T(4,128)(2,1)}), bf16[64,4,128]{2,1,0:T(4,128)(2,1)S(1)}, u32[]{:S(2)}, u32[]{:S(2)}) %all-to-all-start) | async-done | bytes 65568 | tf_op jit(solution)/shard_map/while/body/eval_jaxpr/all_to_all | solution.py:65
  197.5 1.3 collective-permute-start
  198.7 4.9 %collective-permute-start.1 = (bf16[128,1]{1,0:T(8,128)(2,1)S(1)}, bf16[128,1]{1,0:T(8,128)(2,1)S(1)}, u32[]{:S(2)}, u32[]{:S(2)}) collective-permute-start(bf16[128,1]{1,0:T(8,128)(2,1)S(1)} %get-tuple-element.171), channel_id=1, source_target_pairs={{0,1},{1,2},{2,3},{4,5},{5,6},{6,7},{8,9},{9,10},{10,11},{12,13},{... | collective-permute-start | bytes 776 | tf_op jit(solution)/shard_map/while/body/eval_jaxpr/ppermute | solution.py:16
  203.8 1.4 collective-permute-done.1
  208.2 5.5 %all-to-all-start = ((bf16[64,4,128]{2,1,0:T(4,128)(2,1)}), bf16[64,4,128]{2,1,0:T(4,128)(2,1)S(1)}, u32[]{:S(2)}, u32[]{:S(2)}) async-start(bf16[64,4,128]{2,1,0:T(4,128)(2,1)} %broadcast_select_fusion.2), calls=%async_computation | async-start | bytes 131072 | tf_op jit(solution)/shard_map/while/body/eval_jaxpr/all_to_all | solution.py:65
  213.7 8.8 %all-to-all-done = bf16[64,4,128]{2,1,0:T(4,128)(2,1)S(1)} async-done(((bf16[64,4,128]{2,1,0:T(4,128)(2,1)}), bf16[64,4,128]{2,1,0:T(4,128)(2,1)S(1)}, u32[]{:S(2)}, u32[]{:S(2)}) %all-to-all-start) | async-done | bytes 65568 | tf_op jit(solution)/shard_map/while/body/eval_jaxpr/all_to_all | solution.py:65
  223.9 4.6 fusion.28
  230.1 239.7 %all-reduce.3.cloned.1.call-done = f32[8,4096]{1,0:T(8,128)} async-done(((f32[8,4096]{1,0:T(8,128)}), f32[8,4096]{1,0:T(8,128)}) %all-reduce.3.cloned.1.call-update) | async-done | bytes 131088 | tf_op jit(solution)/shard_map/psum | solution.py:88
  469.8 1.3 constant_dynamic-slice_fusion
  (144 shorter events, 30.9 us)
Async XLA Ops:
  7.2 462.6 %all-reduce.3.cloned.1.call-start = ((), (), s32[]{:S(2)}) async-start(), calls=%async_computation.1 | async-start | bytes 262144 | tf_op jit(solution)/shard_map/psum | solution.py:88
  14.4 6.0 %collective-permute-start = (bf16[128,1]{1,0:T(8,128)(2,1)S(1)}, bf16[128,1]{1,0:T(8,128)(2,1)S(1)}, u32[]{:S(2)}, u32[]{:S(2)}) collective-permute-start(bf16[128,1]{1,0:T(8,128)(2,1)S(1)} %get-tuple-element.170), channel_id=1, source_target_pairs={{1,0},{2,1},{3,2},{5,4},{6,5},{7,6},{9,8},{10,9},{11,10},{13,12},{... | collective-permute-start | bytes 776 | tf_op jit(solution)/shard_map/while/body/eval_jaxpr/ppermute | solution.py:19
  15.7 6.1 %collective-permute-start.1 = (bf16[128,1]{1,0:T(8,128)(2,1)S(1)}, bf16[128,1]{1,0:T(8,128)(2,1)S(1)}, u32[]{:S(2)}, u32[]{:S(2)}) collective-permute-start(bf16[128,1]{1,0:T(8,128)(2,1)S(1)} %get-tuple-element.171), channel_id=1, source_target_pairs={{0,1},{1,2},{2,3},{4,5},{5,6},{6,7},{8,9},{9,10},{10,11},{12,13},{... | collective-permute-start | bytes 776 | tf_op jit(solution)/shard_map/while/body/eval_jaxpr/ppermute | solution.py:16
  24.8 20.9 %all-to-all-start = ((bf16[64,4,128]{2,1,0:T(4,128)(2,1)}), bf16[64,4,128]{2,1,0:T(4,128)(2,1)S(1)}, u32[]{:S(2)}, u32[]{:S(2)}) async-start(bf16[64,4,128]{2,1,0:T(4,128)(2,1)} %broadcast_select_fusion.2), calls=%async_computation | async-start | bytes 131072 | tf_op jit(solution)/shard_map/while/body/eval_jaxpr/all_to_all | solution.py:65
  45.9 6.3 %collective-permute-start = (bf16[128,1]{1,0:T(8,128)(2,1)S(1)}, bf16[128,1]{1,0:T(8,128)(2,1)S(1)}, u32[]{:S(2)}, u32[]{:S(2)}) collective-permute-start(bf16[128,1]{1,0:T(8,128)(2,1)S(1)} %get-tuple-element.170), channel_id=1, source_target_pairs={{1,0},{2,1},{3,2},{5,4},{6,5},{7,6},{9,8},{10,9},{11,10},{13,12},{... | collective-permute-start | bytes 776 | tf_op jit(solution)/shard_map/while/body/eval_jaxpr/ppermute | solution.py:19
  47.2 6.4 %collective-permute-start.1 = (bf16[128,1]{1,0:T(8,128)(2,1)S(1)}, bf16[128,1]{1,0:T(8,128)(2,1)S(1)}, u32[]{:S(2)}, u32[]{:S(2)}) collective-permute-start(bf16[128,1]{1,0:T(8,128)(2,1)S(1)} %get-tuple-element.171), channel_id=1, source_target_pairs={{0,1},{1,2},{2,3},{4,5},{5,6},{6,7},{8,9},{9,10},{10,11},{12,13},{... | collective-permute-start | bytes 776 | tf_op jit(solution)/shard_map/while/body/eval_jaxpr/ppermute | solution.py:16
  56.7 14.4 %all-to-all-start = ((bf16[64,4,128]{2,1,0:T(4,128)(2,1)}), bf16[64,4,128]{2,1,0:T(4,128)(2,1)S(1)}, u32[]{:S(2)}, u32[]{:S(2)}) async-start(bf16[64,4,128]{2,1,0:T(4,128)(2,1)} %broadcast_select_fusion.2), calls=%async_computation | async-start | bytes 131072 | tf_op jit(solution)/shard_map/while/body/eval_jaxpr/all_to_all | solution.py:65
  71.2 6.3 %collective-permute-start = (bf16[128,1]{1,0:T(8,128)(2,1)S(1)}, bf16[128,1]{1,0:T(8,128)(2,1)S(1)}, u32[]{:S(2)}, u32[]{:S(2)}) collective-permute-start(bf16[128,1]{1,0:T(8,128)(2,1)S(1)} %get-tuple-element.170), channel_id=1, source_target_pairs={{1,0},{2,1},{3,2},{5,4},{6,5},{7,6},{9,8},{10,9},{11,10},{13,12},{... | collective-permute-start | bytes 776 | tf_op jit(solution)/shard_map/while/body/eval_jaxpr/ppermute | solution.py:19
  72.5 6.4 %collective-permute-start.1 = (bf16[128,1]{1,0:T(8,128)(2,1)S(1)}, bf16[128,1]{1,0:T(8,128)(2,1)S(1)}, u32[]{:S(2)}, u32[]{:S(2)}) collective-permute-start(bf16[128,1]{1,0:T(8,128)(2,1)S(1)} %get-tuple-element.171), channel_id=1, source_target_pairs={{0,1},{1,2},{2,3},{4,5},{5,6},{6,7},{8,9},{9,10},{10,11},{12,13},{... | collective-permute-start | bytes 776 | tf_op jit(solution)/shard_map/while/body/eval_jaxpr/ppermute | solution.py:16
  81.9 14.4 %all-to-all-start = ((bf16[64,4,128]{2,1,0:T(4,128)(2,1)}), bf16[64,4,128]{2,1,0:T(4,128)(2,1)S(1)}, u32[]{:S(2)}, u32[]{:S(2)}) async-start(bf16[64,4,128]{2,1,0:T(4,128)(2,1)} %broadcast_select_fusion.2), calls=%async_computation | async-start | bytes 131072 | tf_op jit(solution)/shard_map/while/body/eval_jaxpr/all_to_all | solution.py:65
  96.4 6.3 %collective-permute-start = (bf16[128,1]{1,0:T(8,128)(2,1)S(1)}, bf16[128,1]{1,0:T(8,128)(2,1)S(1)}, u32[]{:S(2)}, u32[]{:S(2)}) collective-permute-start(bf16[128,1]{1,0:T(8,128)(2,1)S(1)} %get-tuple-element.170), channel_id=1, source_target_pairs={{1,0},{2,1},{3,2},{5,4},{6,5},{7,6},{9,8},{10,9},{11,10},{13,12},{... | collective-permute-start | bytes 776 | tf_op jit(solution)/shard_map/while/body/eval_jaxpr/ppermute | solution.py:19
  97.7 6.4 %collective-permute-start.1 = (bf16[128,1]{1,0:T(8,128)(2,1)S(1)}, bf16[128,1]{1,0:T(8,128)(2,1)S(1)}, u32[]{:S(2)}, u32[]{:S(2)}) collective-permute-start(bf16[128,1]{1,0:T(8,128)(2,1)S(1)} %get-tuple-element.171), channel_id=1, source_target_pairs={{0,1},{1,2},{2,3},{4,5},{5,6},{6,7},{8,9},{9,10},{10,11},{12,13},{... | collective-permute-start | bytes 776 | tf_op jit(solution)/shard_map/while/body/eval_jaxpr/ppermute | solution.py:16
  107.2 14.4 %all-to-all-start = ((bf16[64,4,128]{2,1,0:T(4,128)(2,1)}), bf16[64,4,128]{2,1,0:T(4,128)(2,1)S(1)}, u32[]{:S(2)}, u32[]{:S(2)}) async-start(bf16[64,4,128]{2,1,0:T(4,128)(2,1)} %broadcast_select_fusion.2), calls=%async_computation | async-start | bytes 131072 | tf_op jit(solution)/shard_map/while/body/eval_jaxpr/all_to_all | solution.py:65
  121.7 6.3 %collective-permute-start = (bf16[128,1]{1,0:T(8,128)(2,1)S(1)}, bf16[128,1]{1,0:T(8,128)(2,1)S(1)}, u32[]{:S(2)}, u32[]{:S(2)}) collective-permute-start(bf16[128,1]{1,0:T(8,128)(2,1)S(1)} %get-tuple-element.170), channel_id=1, source_target_pairs={{1,0},{2,1},{3,2},{5,4},{6,5},{7,6},{9,8},{10,9},{11,10},{13,12},{... | collective-permute-start | bytes 776 | tf_op jit(solution)/shard_map/while/body/eval_jaxpr/ppermute | solution.py:19
  123.0 6.4 %collective-permute-start.1 = (bf16[128,1]{1,0:T(8,128)(2,1)S(1)}, bf16[128,1]{1,0:T(8,128)(2,1)S(1)}, u32[]{:S(2)}, u32[]{:S(2)}) collective-permute-start(bf16[128,1]{1,0:T(8,128)(2,1)S(1)} %get-tuple-element.171), channel_id=1, source_target_pairs={{0,1},{1,2},{2,3},{4,5},{5,6},{6,7},{8,9},{9,10},{10,11},{12,13},{... | collective-permute-start | bytes 776 | tf_op jit(solution)/shard_map/while/body/eval_jaxpr/ppermute | solution.py:16
  132.4 14.4 %all-to-all-start = ((bf16[64,4,128]{2,1,0:T(4,128)(2,1)}), bf16[64,4,128]{2,1,0:T(4,128)(2,1)S(1)}, u32[]{:S(2)}, u32[]{:S(2)}) async-start(bf16[64,4,128]{2,1,0:T(4,128)(2,1)} %broadcast_select_fusion.2), calls=%async_computation | async-start | bytes 131072 | tf_op jit(solution)/shard_map/while/body/eval_jaxpr/all_to_all | solution.py:65
  146.9 6.3 %collective-permute-start = (bf16[128,1]{1,0:T(8,128)(2,1)S(1)}, bf16[128,1]{1,0:T(8,128)(2,1)S(1)}, u32[]{:S(2)}, u32[]{:S(2)}) collective-permute-start(bf16[128,1]{1,0:T(8,128)(2,1)S(1)} %get-tuple-element.170), channel_id=1, source_target_pairs={{1,0},{2,1},{3,2},{5,4},{6,5},{7,6},{9,8},{10,9},{11,10},{13,12},{... | collective-permute-start | bytes 776 | tf_op jit(solution)/shard_map/while/body/eval_jaxpr/ppermute | solution.py:19
  148.2 6.4 %collective-permute-start.1 = (bf16[128,1]{1,0:T(8,128)(2,1)S(1)}, bf16[128,1]{1,0:T(8,128)(2,1)S(1)}, u32[]{:S(2)}, u32[]{:S(2)}) collective-permute-start(bf16[128,1]{1,0:T(8,128)(2,1)S(1)} %get-tuple-element.171), channel_id=1, source_target_pairs={{0,1},{1,2},{2,3},{4,5},{5,6},{6,7},{8,9},{9,10},{10,11},{12,13},{... | collective-permute-start | bytes 776 | tf_op jit(solution)/shard_map/while/body/eval_jaxpr/ppermute | solution.py:16
  157.7 14.4 %all-to-all-start = ((bf16[64,4,128]{2,1,0:T(4,128)(2,1)}), bf16[64,4,128]{2,1,0:T(4,128)(2,1)S(1)}, u32[]{:S(2)}, u32[]{:S(2)}) async-start(bf16[64,4,128]{2,1,0:T(4,128)(2,1)} %broadcast_select_fusion.2), calls=%async_computation | async-start | bytes 131072 | tf_op jit(solution)/shard_map/while/body/eval_jaxpr/all_to_all | solution.py:65
  172.2 6.3 %collective-permute-start = (bf16[128,1]{1,0:T(8,128)(2,1)S(1)}, bf16[128,1]{1,0:T(8,128)(2,1)S(1)}, u32[]{:S(2)}, u32[]{:S(2)}) collective-permute-start(bf16[128,1]{1,0:T(8,128)(2,1)S(1)} %get-tuple-element.170), channel_id=1, source_target_pairs={{1,0},{2,1},{3,2},{5,4},{6,5},{7,6},{9,8},{10,9},{11,10},{13,12},{... | collective-permute-start | bytes 776 | tf_op jit(solution)/shard_map/while/body/eval_jaxpr/ppermute | solution.py:19
  173.5 6.4 %collective-permute-start.1 = (bf16[128,1]{1,0:T(8,128)(2,1)S(1)}, bf16[128,1]{1,0:T(8,128)(2,1)S(1)}, u32[]{:S(2)}, u32[]{:S(2)}) collective-permute-start(bf16[128,1]{1,0:T(8,128)(2,1)S(1)} %get-tuple-element.171), channel_id=1, source_target_pairs={{0,1},{1,2},{2,3},{4,5},{5,6},{6,7},{8,9},{9,10},{10,11},{12,13},{... | collective-permute-start | bytes 776 | tf_op jit(solution)/shard_map/while/body/eval_jaxpr/ppermute | solution.py:16
  182.9 14.4 %all-to-all-start = ((bf16[64,4,128]{2,1,0:T(4,128)(2,1)}), bf16[64,4,128]{2,1,0:T(4,128)(2,1)S(1)}, u32[]{:S(2)}, u32[]{:S(2)}) async-start(bf16[64,4,128]{2,1,0:T(4,128)(2,1)} %broadcast_select_fusion.2), calls=%async_computation | async-start | bytes 131072 | tf_op jit(solution)/shard_map/while/body/eval_jaxpr/all_to_all | solution.py:65
  197.5 6.3 %collective-permute-start = (bf16[128,1]{1,0:T(8,128)(2,1)S(1)}, bf16[128,1]{1,0:T(8,128)(2,1)S(1)}, u32[]{:S(2)}, u32[]{:S(2)}) collective-permute-start(bf16[128,1]{1,0:T(8,128)(2,1)S(1)} %get-tuple-element.170), channel_id=1, source_target_pairs={{1,0},{2,1},{3,2},{5,4},{6,5},{7,6},{9,8},{10,9},{11,10},{13,12},{... | collective-permute-start | bytes 776 | tf_op jit(solution)/shard_map/while/body/eval_jaxpr/ppermute | solution.py:19
  198.7 6.4 %collective-permute-start.1 = (bf16[128,1]{1,0:T(8,128)(2,1)S(1)}, bf16[128,1]{1,0:T(8,128)(2,1)S(1)}, u32[]{:S(2)}, u32[]{:S(2)}) collective-permute-start(bf16[128,1]{1,0:T(8,128)(2,1)S(1)} %get-tuple-element.171), channel_id=1, source_target_pairs={{0,1},{1,2},{2,3},{4,5},{5,6},{6,7},{8,9},{9,10},{10,11},{12,13},{... | collective-permute-start | bytes 776 | tf_op jit(solution)/shard_map/while/body/eval_jaxpr/ppermute | solution.py:16
  208.2 14.4 %all-to-all-start = ((bf16[64,4,128]{2,1,0:T(4,128)(2,1)}), bf16[64,4,128]{2,1,0:T(4,128)(2,1)S(1)}, u32[]{:S(2)}, u32[]{:S(2)}) async-start(bf16[64,4,128]{2,1,0:T(4,128)(2,1)} %broadcast_select_fusion.2), calls=%async_computation | async-start | bytes 131072 | tf_op jit(solution)/shard_map/while/body/eval_jaxpr/all_to_all | solution.py:65
  222.6 248.6 %copy-start = (f32[128,128]{1,0:T(8,128)}, f32[128,128]{1,0:T(8,128)S(1)}, u32[]{:S(2)}) copy-start(f32[128,128]{1,0:T(8,128)S(1)} %get-tuple-element.81) | copy-start | bytes 196612
  222.6 6.0 %copy-start.1 = (s32[1,128,2]{1,2,0:T(2,128)S(1)}, s32[1,128,2]{1,2,0:T(2,128)}, u32[]{:S(2)}) copy-start(s32[1,128,2]{1,2,0:T(2,128)} %param.18) | copy-start | bytes 3076
Sparse Core Ops, SparseCore 0:
  230.2 239.5 all-reduce.2
where the time goes:
time: 480 us; the launch traced here: 478 us
  waiting for transfers between devices  322 us (67%)
  starting transfers between devices  99.5 us (21%)
  matrix products  15.6 us (3%)
  local copies, waits for them, and re-layouts  14.6 us (3%)
  between operations  14.1 us (3%)
  other arithmetic  11.6 us (2%)
    psum x1, waiting for transfers between devices, on_device(): summed = lax.psum(partial_sum, ('tile', 'sec'))  240 us
    all_to_all x8, waiting for transfers between devices, advance_send(): lax.all_to_all(outgoing, 'tile', split_axis=0, concat_axis=0, tiled=True)  70.7 us
    all_to_all x8, starting transfers between devices, advance_send(): lax.all_to_all(outgoing, 'tile', split_axis=0, concat_axis=0, tiled=True)  50.7 us
    ppermute x8, starting transfers between devices, padded_2(): lax.ppermute(lax.slice_in_dim(block, block.shape[dim] - width, None, axis...  38.5 us
    ppermute x8, waiting for transfers between devices, padded_2(): lax.ppermute(lax.slice_in_dim(block, block.shape[dim] - width, None, axis...  11.2 us
    ppermute x8, starting transfers between devices, padded_2(): lax.ppermute(lax.slice_in_dim(block, 0, width, axis=dim), axis, backward)  10.3 us
    dot_general x8, matrix products, cable_update(): jnp.einsum('ci,ji->cj', right_side, inv_cable, precision=lax.Precision.HI...  10.2 us
  transfers between devices with their start and end apart: 25, of which 17 were waited for; matrix products, arithmetic and copies ran while one was open for 0% of the time, Pallas kernels for 0%

commit v1 on v0

--- a/solution.py
+++ b/solution.py
@@ -85,7 +85,7 @@
     )
     partial_sum = jnp.einsum("tskc,skq->tqc", tile_sums, select, precision=lax.Precision.HIGHEST)
     partial_sum = partial_sum.reshape(step_count, tile_total * contact_width)
-    summed = lax.psum(partial_sum, ("tile", "sec"))
+    summed = lax.psum(lax.psum(partial_sum, "sec"), "tile")
     share_width = summed.shape[1] // (tile_count * section_count)
     position = lax.axis_index("tile") * section_count + lax.axis_index("sec")
     probe_share = lax.dynamic_slice_in_dim(summed, position * share_width, share_width, 1)

time: 480 us -> 463 us (0.965)
  waiting for transfers between devices: 322 us -> 302 us
    psum x1 -> x2, waiting for transfers between devices: 240 us -> 220 us  [on_device(): summed = lax.psum(lax.psum(partial_sum, 'sec'), 'tile')]
  transfers between devices with their start and end apart: 25 -> 26, of which waited for: 17 -> 18; matrix products, arithmetic and copies ran while one was open for 0% -> 0% of each run, Pallas kernels for 0% -> 0%
where the time goes in v1:
time: 463 us; the launch traced here: 459 us
  waiting for transfers between devices  302 us (65%)
  starting transfers between devices  99.5 us (21%)
  matrix products  15.6 us (3%)
  local copies, waits for them, and re-layouts  14.6 us (3%)
  between operations  14.1 us (3%)
  other arithmetic  11.6 us (3%)
    psum x2, waiting for transfers between devices, on_device(): summed = lax.psum(lax.psum(partial_sum, 'sec'), 'tile')  220 us
    all_to_all x8, waiting for transfers between devices, advance_send(): lax.all_to_all(outgoing, 'tile', split_axis=0, concat_axis=0, tiled=True)  70.7 us
    all_to_all x8, starting transfers between devices, advance_send(): lax.all_to_all(outgoing, 'tile', split_axis=0, concat_axis=0, tiled=True)  50.6 us
    ppermute x8, starting transfers between devices, padded_2(): lax.ppermute(lax.slice_in_dim(block, block.shape[dim] - width, None, axis...  38.5 us
    ppermute x8, waiting for transfers between devices, padded_2(): lax.ppermute(lax.slice_in_dim(block, block.shape[dim] - width, None, axis...  11.2 us
    ppermute x8, starting transfers between devices, padded_2(): lax.ppermute(lax.slice_in_dim(block, 0, width, axis=dim), axis, backward)  10.3 us
    dot_general x8, matrix products, cable_update(): jnp.einsum('ci,ji->cj', right_side, inv_cable, precision=lax.Precision.HI...  10.2 us
  transfers between devices with their start and end apart: 26, of which 18 were waited for; matrix products, arithmetic and copies ran while one was open for 0% of the time, Pallas kernels for 0%

profile of v1, /device:TPU:8, one launch (start us, length us, event | category | flops | bytes accessed | tf_op | source)
XLA Modules:
  0.0 458.6 jit_solution(12587647744360017392)
XLA Ops:
  14.3 208.3 %while.13 = (s32[]{:T(128)}, f32[128,128]{1,0:T(8,128)S(1)}, bf16[8,64,4,128]{3,2,1,0:T(4,128)(2,1)S(1)}, f32[128,128]{1,0:T(8,128)}, bf16[8,128,128]{2,1,0:T(8,...) while((s32[]{:T(128)}, f32[128,128]{1,0:T(8,128)S(1)}, ...), condition=%wide.region_4.5_spmd, body=%wide.region_3.4_spmd.sunk | while | flops 25629952 | bytes 1626603 | solution.py:68
  14.4 1.3 collective-permute-start
  15.7 4.5 collective-permute-start.1
  20.4 1.4 collective-permute-done.1
  24.8 12.1 %all-to-all-start = ((bf16[64,4,128]{2,1,0:T(4,128)(2,1)}), bf16[64,4,128]{2,1,0:T(4,128)(2,1)S(1)}, u32[]{:S(2)}, u32[]{:S(2)}) async-start(bf16[64,4,128]{2,1,0:T(4,128)(2,1)} %broadcast_select_fusion.2), calls=%async_computation | async-start | bytes 131072 | tf_op jit(solution)/shard_map/while/body/eval_jaxpr/all_to_all | solution.py:65
  36.9 8.8 %all-to-all-done = bf16[64,4,128]{2,1,0:T(4,128)(2,1)S(1)} async-done(((bf16[64,4,128]{2,1,0:T(4,128)(2,1)}), bf16[64,4,128]{2,1,0:T(4,128)(2,1)S(1)}, u32[]{:S(2)}, u32[]{:S(2)}) %all-to-all-start) | async-done | bytes 65568 | tf_op jit(solution)/shard_map/while/body/eval_jaxpr/all_to_all | solution.py:65
  45.9 1.3 collective-permute-start
  47.2 4.9 %collective-permute-start.1 = (bf16[128,1]{1,0:T(8,128)(2,1)S(1)}, bf16[128,1]{1,0:T(8,128)(2,1)S(1)}, u32[]{:S(2)}, u32[]{:S(2)}) collective-permute-start(bf16[128,1]{1,0:T(8,128)(2,1)S(1)} %get-tuple-element.171), channel_id=1, source_target_pairs={{0,1},{1,2},{2,3},{4,5},{5,6},{6,7},{8,9},{9,10},{10,11},{12,13},{... | collective-permute-start | bytes 776 | tf_op jit(solution)/shard_map/while/body/eval_jaxpr/ppermute | solution.py:16
  52.2 1.4 collective-permute-done.1
  56.7 5.5 %all-to-all-start = ((bf16[64,4,128]{2,1,0:T(4,128)(2,1)}), bf16[64,4,128]{2,1,0:T(4,128)(2,1)S(1)}, u32[]{:S(2)}, u32[]{:S(2)}) async-start(bf16[64,4,128]{2,1,0:T(4,128)(2,1)} %broadcast_select_fusion.2), calls=%async_computation | async-start | bytes 131072 | tf_op jit(solution)/shard_map/while/body/eval_jaxpr/all_to_all | solution.py:65
  62.2 8.8 %all-to-all-done = bf16[64,4,128]{2,1,0:T(4,128)(2,1)S(1)} async-done(((bf16[64,4,128]{2,1,0:T(4,128)(2,1)}), bf16[64,4,128]{2,1,0:T(4,128)(2,1)S(1)}, u32[]{:S(2)}, u32[]{:S(2)}) %all-to-all-start) | async-done | bytes 65568 | tf_op jit(solution)/shard_map/while/body/eval_jaxpr/all_to_all | solution.py:65
  71.2 1.3 collective-permute-start
  72.5 4.9 %collective-permute-start.1 = (bf16[128,1]{1,0:T(8,128)(2,1)S(1)}, bf16[128,1]{1,0:T(8,128)(2,1)S(1)}, u32[]{:S(2)}, u32[]{:S(2)}) collective-permute-start(bf16[128,1]{1,0:T(8,128)(2,1)S(1)} %get-tuple-element.171), channel_id=1, source_target_pairs={{0,1},{1,2},{2,3},{4,5},{5,6},{6,7},{8,9},{9,10},{10,11},{12,13},{... | collective-permute-start | bytes 776 | tf_op jit(solution)/shard_map/while/body/eval_jaxpr/ppermute | solution.py:16
  77.5 1.4 collective-permute-done.1
  81.9 5.5 %all-to-all-start = ((bf16[64,4,128]{2,1,0:T(4,128)(2,1)}), bf16[64,4,128]{2,1,0:T(4,128)(2,1)S(1)}, u32[]{:S(2)}, u32[]{:S(2)}) async-start(bf16[64,4,128]{2,1,0:T(4,128)(2,1)} %broadcast_select_fusion.2), calls=%async_computation | async-start | bytes 131072 | tf_op jit(solution)/shard_map/while/body/eval_jaxpr/all_to_all | solution.py:65
  87.4 8.8 %all-to-all-done = bf16[64,4,128]{2,1,0:T(4,128)(2,1)S(1)} async-done(((bf16[64,4,128]{2,1,0:T(4,128)(2,1)}), bf16[64,4,128]{2,1,0:T(4,128)(2,1)S(1)}, u32[]{:S(2)}, u32[]{:S(2)}) %all-to-all-start) | async-done | bytes 65568 | tf_op jit(solution)/shard_map/while/body/eval_jaxpr/all_to_all | solution.py:65
  96.4 1.3 collective-permute-start
  97.7 4.9 %collective-permute-start.1 = (bf16[128,1]{1,0:T(8,128)(2,1)S(1)}, bf16[128,1]{1,0:T(8,128)(2,1)S(1)}, u32[]{:S(2)}, u32[]{:S(2)}) collective-permute-start(bf16[128,1]{1,0:T(8,128)(2,1)S(1)} %get-tuple-element.171), channel_id=1, source_target_pairs={{0,1},{1,2},{2,3},{4,5},{5,6},{6,7},{8,9},{9,10},{10,11},{12,13},{... | collective-permute-start | bytes 776 | tf_op jit(solution)/shard_map/while/body/eval_jaxpr/ppermute | solution.py:16
  102.8 1.4 collective-permute-done.1
  104.3 1.3 fusion.52
  107.2 5.5 %all-to-all-start = ((bf16[64,4,128]{2,1,0:T(4,128)(2,1)}), bf16[64,4,128]{2,1,0:T(4,128)(2,1)S(1)}, u32[]{:S(2)}, u32[]{:S(2)}) async-start(bf16[64,4,128]{2,1,0:T(4,128)(2,1)} %broadcast_select_fusion.2), calls=%async_computation | async-start | bytes 131072 | tf_op jit(solution)/shard_map/while/body/eval_jaxpr/all_to_all | solution.py:65
  112.7 8.8 %all-to-all-done = bf16[64,4,128]{2,1,0:T(4,128)(2,1)S(1)} async-done(((bf16[64,4,128]{2,1,0:T(4,128)(2,1)}), bf16[64,4,128]{2,1,0:T(4,128)(2,1)S(1)}, u32[]{:S(2)}, u32[]{:S(2)}) %all-to-all-start) | async-done | bytes 65568 | tf_op jit(solution)/shard_map/while/body/eval_jaxpr/all_to_all | solution.py:65
  121.7 1.3 collective-permute-start
  123.0 4.8 %collective-permute-start.1 = (bf16[128,1]{1,0:T(8,128)(2,1)S(1)}, bf16[128,1]{1,0:T(8,128)(2,1)S(1)}, u32[]{:S(2)}, u32[]{:S(2)}) collective-permute-start(bf16[128,1]{1,0:T(8,128)(2,1)S(1)} %get-tuple-element.171), channel_id=1, source_target_pairs={{0,1},{1,2},{2,3},{4,5},{5,6},{6,7},{8,9},{9,10},{10,11},{12,13},{... | collective-permute-start | bytes 776 | tf_op jit(solution)/shard_map/while/body/eval_jaxpr/ppermute | solution.py:16
  128.0 1.4 collective-permute-done.1
  132.4 5.5 %all-to-all-start = ((bf16[64,4,128]{2,1,0:T(4,128)(2,1)}), bf16[64,4,128]{2,1,0:T(4,128)(2,1)S(1)}, u32[]{:S(2)}, u32[]{:S(2)}) async-start(bf16[64,4,128]{2,1,0:T(4,128)(2,1)} %broadcast_select_fusion.2), calls=%async_computation | async-start | bytes 131072 | tf_op jit(solution)/shard_map/while/body/eval_jaxpr/all_to_all | solution.py:65
  137.9 8.8 %all-to-all-done = bf16[64,4,128]{2,1,0:T(4,128)(2,1)S(1)} async-done(((bf16[64,4,128]{2,1,0:T(4,128)(2,1)}), bf16[64,4,128]{2,1,0:T(4,128)(2,1)S(1)}, u32[]{:S(2)}, u32[]{:S(2)}) %all-to-all-start) | async-done | bytes 65568 | tf_op jit(solution)/shard_map/while/body/eval_jaxpr/all_to_all | solution.py:65
  146.9 1.3 collective-permute-start
  148.2 4.9 %collective-permute-start.1 = (bf16[128,1]{1,0:T(8,128)(2,1)S(1)}, bf16[128,1]{1,0:T(8,128)(2,1)S(1)}, u32[]{:S(2)}, u32[]{:S(2)}) collective-permute-start(bf16[128,1]{1,0:T(8,128)(2,1)S(1)} %get-tuple-element.171), channel_id=1, source_target_pairs={{0,1},{1,2},{2,3},{4,5},{5,6},{6,7},{8,9},{9,10},{10,11},{12,13},{... | collective-permute-start | bytes 776 | tf_op jit(solution)/shard_map/while/body/eval_jaxpr/ppermute | solution.py:16
  153.3 1.4 collective-permute-done.1
  154.8 1.3 fusion.52
  157.7 5.5 %all-to-all-start = ((bf16[64,4,128]{2,1,0:T(4,128)(2,1)}), bf16[64,4,128]{2,1,0:T(4,128)(2,1)S(1)}, u32[]{:S(2)}, u32[]{:S(2)}) async-start(bf16[64,4,128]{2,1,0:T(4,128)(2,1)} %broadcast_select_fusion.2), calls=%async_computation | async-start | bytes 131072 | tf_op jit(solution)/shard_map/while/body/eval_jaxpr/all_to_all | solution.py:65
  163.2 8.8 %all-to-all-done = bf16[64,4,128]{2,1,0:T(4,128)(2,1)S(1)} async-done(((bf16[64,4,128]{2,1,0:T(4,128)(2,1)}), bf16[64,4,128]{2,1,0:T(4,128)(2,1)S(1)}, u32[]{:S(2)}, u32[]{:S(2)}) %all-to-all-start) | async-done | bytes 65568 | tf_op jit(solution)/shard_map/while/body/eval_jaxpr/all_to_all | solution.py:65
  172.2 1.3 collective-permute-start
  173.5 4.9 %collective-permute-start.1 = (bf16[128,1]{1,0:T(8,128)(2,1)S(1)}, bf16[128,1]{1,0:T(8,128)(2,1)S(1)}, u32[]{:S(2)}, u32[]{:S(2)}) collective-permute-start(bf16[128,1]{1,0:T(8,128)(2,1)S(1)} %get-tuple-element.171), channel_id=1, source_target_pairs={{0,1},{1,2},{2,3},{4,5},{5,6},{6,7},{8,9},{9,10},{10,11},{12,13},{... | collective-permute-start | bytes 776 | tf_op jit(solution)/shard_map/while/body/eval_jaxpr/ppermute | solution.py:16
  178.5 1.4 collective-permute-done.1
  180.0 1.3 fusion.52
  182.9 5.5 %all-to-all-start = ((bf16[64,4,128]{2,1,0:T(4,128)(2,1)}), bf16[64,4,128]{2,1,0:T(4,128)(2,1)S(1)}, u32[]{:S(2)}, u32[]{:S(2)}) async-start(bf16[64,4,128]{2,1,0:T(4,128)(2,1)} %broadcast_select_fusion.2), calls=%async_computation | async-start | bytes 131072 | tf_op jit(solution)/shard_map/while/body/eval_jaxpr/all_to_all | solution.py:65
  188.4 8.8 %all-to-all-done = bf16[64,4,128]{2,1,0:T(4,128)(2,1)S(1)} async-done(((bf16[64,4,128]{2,1,0:T(4,128)(2,1)}), bf16[64,4,128]{2,1,0:T(4,128)(2,1)S(1)}, u32[]{:S(2)}, u32[]{:S(2)}) %all-to-all-start) | async-done | bytes 65568 | tf_op jit(solution)/shard_map/while/body/eval_jaxpr/all_to_all | solution.py:65
  197.4 1.3 collective-permute-start
  198.7 4.8 %collective-permute-start.1 = (bf16[128,1]{1,0:T(8,128)(2,1)S(1)}, bf16[128,1]{1,0:T(8,128)(2,1)S(1)}, u32[]{:S(2)}, u32[]{:S(2)}) collective-permute-start(bf16[128,1]{1,0:T(8,128)(2,1)S(1)} %get-tuple-element.171), channel_id=1, source_target_pairs={{0,1},{1,2},{2,3},{4,5},{5,6},{6,7},{8,9},{9,10},{10,11},{12,13},{... | collective-permute-start | bytes 776 | tf_op jit(solution)/shard_map/while/body/eval_jaxpr/ppermute | solution.py:16
  203.8 1.4 collective-permute-done.1
  208.2 5.5 %all-to-all-start = ((bf16[64,4,128]{2,1,0:T(4,128)(2,1)}), bf16[64,4,128]{2,1,0:T(4,128)(2,1)S(1)}, u32[]{:S(2)}, u32[]{:S(2)}) async-start(bf16[64,4,128]{2,1,0:T(4,128)(2,1)} %broadcast_select_fusion.2), calls=%async_computation | async-start | bytes 131072 | tf_op jit(solution)/shard_map/while/body/eval_jaxpr/all_to_all | solution.py:65
  213.7 8.8 %all-to-all-done = bf16[64,4,128]{2,1,0:T(4,128)(2,1)S(1)} async-done(((bf16[64,4,128]{2,1,0:T(4,128)(2,1)}), bf16[64,4,128]{2,1,0:T(4,128)(2,1)S(1)}, u32[]{:S(2)}, u32[]{:S(2)}) %all-to-all-start) | async-done | bytes 65568 | tf_op jit(solution)/shard_map/while/body/eval_jaxpr/all_to_all | solution.py:65
  223.9 4.6 %fusion.28 = f32[8,128,2,128]{3,0,2,1:T(8,128)S(1)} fusion(bf16[1,128,2,128,128]{4,3,2,1,0:T(8,128)(2,1)} %param.19, bf16[128,8,128]{2,1,0:T(8,128)(2,1)S(1)} %gather_fusion.1, pred[128]{0:T(512)(128)(4,1)S(1)} %compare_and_fusion.1), kind=kOutput, calls=%fused_computation.41 | convolution fusion | flops 67239936 | bytes 9699456 | tf_op jit(solution)/shard_map/tsi,skic->tskc/dot_general | solution.py:82
  230.1 44.0 %all-reduce.4.cloned.1.call-done = f32[8,4096]{1,0:T(8,128)} async-done(((f32[8,4096]{1,0:T(8,128)}), f32[8,4096]{1,0:T(8,128)}) %all-reduce.4.cloned.1.call-update) | async-done | bytes 131088 | tf_op jit(solution)/shard_map/psum | solution.py:88
  274.2 176.3 %all-reduce.6.cloned.1.call-done = f32[8,4096]{1,0:T(8,128)} async-done(((f32[8,4096]{1,0:T(8,128)}), f32[8,4096]{1,0:T(8,128)}) %all-reduce.6.cloned.1.call-update) | async-done | bytes 131088 | tf_op jit(solution)/shard_map/psum | solution.py:88
  450.5 1.3 constant_dynamic-slice_fusion
  (147 shorter events, 32.2 us)
Async XLA Ops:
  7.2 267.0 %all-reduce.4.cloned.1.call-start = ((), (), s32[]{:S(2)}) async-start(), calls=%async_computation.1 | async-start | bytes 262144 | tf_op jit(solution)/shard_map/psum | solution.py:88
  14.4 6.0 %collective-permute-start = (bf16[128,1]{1,0:T(8,128)(2,1)S(1)}, bf16[128,1]{1,0:T(8,128)(2,1)S(1)}, u32[]{:S(2)}, u32[]{:S(2)}) collective-permute-start(bf16[128,1]{1,0:T(8,128)(2,1)S(1)} %get-tuple-element.170), channel_id=1, source_target_pairs={{1,0},{2,1},{3,2},{5,4},{6,5},{7,6},{9,8},{10,9},{11,10},{13,12},{... | collective-permute-start | bytes 776 | tf_op jit(solution)/shard_map/while/body/eval_jaxpr/ppermute | solution.py:19
  15.7 6.1 %collective-permute-start.1 = (bf16[128,1]{1,0:T(8,128)(2,1)S(1)}, bf16[128,1]{1,0:T(8,128)(2,1)S(1)}, u32[]{:S(2)}, u32[]{:S(2)}) collective-permute-start(bf16[128,1]{1,0:T(8,128)(2,1)S(1)} %get-tuple-element.171), channel_id=1, source_target_pairs={{0,1},{1,2},{2,3},{4,5},{5,6},{6,7},{8,9},{9,10},{10,11},{12,13},{... | collective-permute-start | bytes 776 | tf_op jit(solution)/shard_map/while/body/eval_jaxpr/ppermute | solution.py:16
  24.8 20.9 %all-to-all-start = ((bf16[64,4,128]{2,1,0:T(4,128)(2,1)}), bf16[64,4,128]{2,1,0:T(4,128)(2,1)S(1)}, u32[]{:S(2)}, u32[]{:S(2)}) async-start(bf16[64,4,128]{2,1,0:T(4,128)(2,1)} %broadcast_select_fusion.2), calls=%async_computation | async-start | bytes 131072 | tf_op jit(solution)/shard_map/while/body/eval_jaxpr/all_to_all | solution.py:65
  45.9 6.3 %collective-permute-start = (bf16[128,1]{1,0:T(8,128)(2,1)S(1)}, bf16[128,1]{1,0:T(8,128)(2,1)S(1)}, u32[]{:S(2)}, u32[]{:S(2)}) collective-permute-start(bf16[128,1]{1,0:T(8,128)(2,1)S(1)} %get-tuple-element.170), channel_id=1, source_target_pairs={{1,0},{2,1},{3,2},{5,4},{6,5},{7,6},{9,8},{10,9},{11,10},{13,12},{... | collective-permute-start | bytes 776 | tf_op jit(solution)/shard_map/while/body/eval_jaxpr/ppermute | solution.py:19
  47.2 6.4 %collective-permute-start.1 = (bf16[128,1]{1,0:T(8,128)(2,1)S(1)}, bf16[128,1]{1,0:T(8,128)(2,1)S(1)}, u32[]{:S(2)}, u32[]{:S(2)}) collective-permute-start(bf16[128,1]{1,0:T(8,128)(2,1)S(1)} %get-tuple-element.171), channel_id=1, source_target_pairs={{0,1},{1,2},{2,3},{4,5},{5,6},{6,7},{8,9},{9,10},{10,11},{12,13},{... | collective-permute-start | bytes 776 | tf_op jit(solution)/shard_map/while/body/eval_jaxpr/ppermute | solution.py:16
  56.7 14.4 %all-to-all-start = ((bf16[64,4,128]{2,1,0:T(4,128)(2,1)}), bf16[64,4,128]{2,1,0:T(4,128)(2,1)S(1)}, u32[]{:S(2)}, u32[]{:S(2)}) async-start(bf16[64,4,128]{2,1,0:T(4,128)(2,1)} %broadcast_select_fusion.2), calls=%async_computation | async-start | bytes 131072 | tf_op jit(solution)/shard_map/while/body/eval_jaxpr/all_to_all | solution.py:65
  71.2 6.3 %collective-permute-start = (bf16[128,1]{1,0:T(8,128)(2,1)S(1)}, bf16[128,1]{1,0:T(8,128)(2,1)S(1)}, u32[]{:S(2)}, u32[]{:S(2)}) collective-permute-start(bf16[128,1]{1,0:T(8,128)(2,1)S(1)} %get-tuple-element.170), channel_id=1, source_target_pairs={{1,0},{2,1},{3,2},{5,4},{6,5},{7,6},{9,8},{10,9},{11,10},{13,12},{... | collective-permute-start | bytes 776 | tf_op jit(solution)/shard_map/while/body/eval_jaxpr/ppermute | solution.py:19
  72.5 6.4 %collective-permute-start.1 = (bf16[128,1]{1,0:T(8,128)(2,1)S(1)}, bf16[128,1]{1,0:T(8,128)(2,1)S(1)}, u32[]{:S(2)}, u32[]{:S(2)}) collective-permute-start(bf16[128,1]{1,0:T(8,128)(2,1)S(1)} %get-tuple-element.171), channel_id=1, source_target_pairs={{0,1},{1,2},{2,3},{4,5},{5,6},{6,7},{8,9},{9,10},{10,11},{12,13},{... | collective-permute-start | bytes 776 | tf_op jit(solution)/shard_map/while/body/eval_jaxpr/ppermute | solution.py:16
  81.9 14.3 %all-to-all-start = ((bf16[64,4,128]{2,1,0:T(4,128)(2,1)}), bf16[64,4,128]{2,1,0:T(4,128)(2,1)S(1)}, u32[]{:S(2)}, u32[]{:S(2)}) async-start(bf16[64,4,128]{2,1,0:T(4,128)(2,1)} %broadcast_select_fusion.2), calls=%async_computation | async-start | bytes 131072 | tf_op jit(solution)/shard_map/while/body/eval_jaxpr/all_to_all | solution.py:65
  96.4 6.3 %collective-permute-start = (bf16[128,1]{1,0:T(8,128)(2,1)S(1)}, bf16[128,1]{1,0:T(8,128)(2,1)S(1)}, u32[]{:S(2)}, u32[]{:S(2)}) collective-permute-start(bf16[128,1]{1,0:T(8,128)(2,1)S(1)} %get-tuple-element.170), channel_id=1, source_target_pairs={{1,0},{2,1},{3,2},{5,4},{6,5},{7,6},{9,8},{10,9},{11,10},{13,12},{... | collective-permute-start | bytes 776 | tf_op jit(solution)/shard_map/while/body/eval_jaxpr/ppermute | solution.py:19
  97.7 6.4 %collective-permute-start.1 = (bf16[128,1]{1,0:T(8,128)(2,1)S(1)}, bf16[128,1]{1,0:T(8,128)(2,1)S(1)}, u32[]{:S(2)}, u32[]{:S(2)}) collective-permute-start(bf16[128,1]{1,0:T(8,128)(2,1)S(1)} %get-tuple-element.171), channel_id=1, source_target_pairs={{0,1},{1,2},{2,3},{4,5},{5,6},{6,7},{8,9},{9,10},{10,11},{12,13},{... | collective-permute-start | bytes 776 | tf_op jit(solution)/shard_map/while/body/eval_jaxpr/ppermute | solution.py:16
  107.2 14.3 %all-to-all-start = ((bf16[64,4,128]{2,1,0:T(4,128)(2,1)}), bf16[64,4,128]{2,1,0:T(4,128)(2,1)S(1)}, u32[]{:S(2)}, u32[]{:S(2)}) async-start(bf16[64,4,128]{2,1,0:T(4,128)(2,1)} %broadcast_select_fusion.2), calls=%async_computation | async-start | bytes 131072 | tf_op jit(solution)/shard_map/while/body/eval_jaxpr/all_to_all | solution.py:65
  121.7 6.3 %collective-permute-start = (bf16[128,1]{1,0:T(8,128)(2,1)S(1)}, bf16[128,1]{1,0:T(8,128)(2,1)S(1)}, u32[]{:S(2)}, u32[]{:S(2)}) collective-permute-start(bf16[128,1]{1,0:T(8,128)(2,1)S(1)} %get-tuple-element.170), channel_id=1, source_target_pairs={{1,0},{2,1},{3,2},{5,4},{6,5},{7,6},{9,8},{10,9},{11,10},{13,12},{... | collective-permute-start | bytes 776 | tf_op jit(solution)/shard_map/while/body/eval_jaxpr/ppermute | solution.py:19
  123.0 6.4 %collective-permute-start.1 = (bf16[128,1]{1,0:T(8,128)(2,1)S(1)}, bf16[128,1]{1,0:T(8,128)(2,1)S(1)}, u32[]{:S(2)}, u32[]{:S(2)}) collective-permute-start(bf16[128,1]{1,0:T(8,128)(2,1)S(1)} %get-tuple-element.171), channel_id=1, source_target_pairs={{0,1},{1,2},{2,3},{4,5},{5,6},{6,7},{8,9},{9,10},{10,11},{12,13},{... | collective-permute-start | bytes 776 | tf_op jit(solution)/shard_map/while/body/eval_jaxpr/ppermute | solution.py:16
  132.4 14.4 %all-to-all-start = ((bf16[64,4,128]{2,1,0:T(4,128)(2,1)}), bf16[64,4,128]{2,1,0:T(4,128)(2,1)S(1)}, u32[]{:S(2)}, u32[]{:S(2)}) async-start(bf16[64,4,128]{2,1,0:T(4,128)(2,1)} %broadcast_select_fusion.2), calls=%async_computation | async-start | bytes 131072 | tf_op jit(solution)/shard_map/while/body/eval_jaxpr/all_to_all | solution.py:65
  146.9 6.3 %collective-permute-start = (bf16[128,1]{1,0:T(8,128)(2,1)S(1)}, bf16[128,1]{1,0:T(8,128)(2,1)S(1)}, u32[]{:S(2)}, u32[]{:S(2)}) collective-permute-start(bf16[128,1]{1,0:T(8,128)(2,1)S(1)} %get-tuple-element.170), channel_id=1, source_target_pairs={{1,0},{2,1},{3,2},{5,4},{6,5},{7,6},{9,8},{10,9},{11,10},{13,12},{... | collective-permute-start | bytes 776 | tf_op jit(solution)/shard_map/while/body/eval_jaxpr/ppermute | solution.py:19
  148.2 6.4 %collective-permute-start.1 = (bf16[128,1]{1,0:T(8,128)(2,1)S(1)}, bf16[128,1]{1,0:T(8,128)(2,1)S(1)}, u32[]{:S(2)}, u32[]{:S(2)}) collective-permute-start(bf16[128,1]{1,0:T(8,128)(2,1)S(1)} %get-tuple-element.171), channel_id=1, source_target_pairs={{0,1},{1,2},{2,3},{4,5},{5,6},{6,7},{8,9},{9,10},{10,11},{12,13},{... | collective-permute-start | bytes 776 | tf_op jit(solution)/shard_map/while/body/eval_jaxpr/ppermute | solution.py:16
  157.7 14.3 %all-to-all-start = ((bf16[64,4,128]{2,1,0:T(4,128)(2,1)}), bf16[64,4,128]{2,1,0:T(4,128)(2,1)S(1)}, u32[]{:S(2)}, u32[]{:S(2)}) async-start(bf16[64,4,128]{2,1,0:T(4,128)(2,1)} %broadcast_select_fusion.2), calls=%async_computation | async-start | bytes 131072 | tf_op jit(solution)/shard_map/while/body/eval_jaxpr/all_to_all | solution.py:65
  172.2 6.3 %collective-permute-start = (bf16[128,1]{1,0:T(8,128)(2,1)S(1)}, bf16[128,1]{1,0:T(8,128)(2,1)S(1)}, u32[]{:S(2)}, u32[]{:S(2)}) collective-permute-start(bf16[128,1]{1,0:T(8,128)(2,1)S(1)} %get-tuple-element.170), channel_id=1, source_target_pairs={{1,0},{2,1},{3,2},{5,4},{6,5},{7,6},{9,8},{10,9},{11,10},{13,12},{... | collective-permute-start | bytes 776 | tf_op jit(solution)/shard_map/while/body/eval_jaxpr/ppermute | solution.py:19
  173.5 6.4 %collective-permute-start.1 = (bf16[128,1]{1,0:T(8,128)(2,1)S(1)}, bf16[128,1]{1,0:T(8,128)(2,1)S(1)}, u32[]{:S(2)}, u32[]{:S(2)}) collective-permute-start(bf16[128,1]{1,0:T(8,128)(2,1)S(1)} %get-tuple-element.171), channel_id=1, source_target_pairs={{0,1},{1,2},{2,3},{4,5},{5,6},{6,7},{8,9},{9,10},{10,11},{12,13},{... | collective-permute-start | bytes 776 | tf_op jit(solution)/shard_map/while/body/eval_jaxpr/ppermute | solution.py:16
  182.9 14.3 %all-to-all-start = ((bf16[64,4,128]{2,1,0:T(4,128)(2,1)}), bf16[64,4,128]{2,1,0:T(4,128)(2,1)S(1)}, u32[]{:S(2)}, u32[]{:S(2)}) async-start(bf16[64,4,128]{2,1,0:T(4,128)(2,1)} %broadcast_select_fusion.2), calls=%async_computation | async-start | bytes 131072 | tf_op jit(solution)/shard_map/while/body/eval_jaxpr/all_to_all | solution.py:65
  197.4 6.3 %collective-permute-start = (bf16[128,1]{1,0:T(8,128)(2,1)S(1)}, bf16[128,1]{1,0:T(8,128)(2,1)S(1)}, u32[]{:S(2)}, u32[]{:S(2)}) collective-permute-start(bf16[128,1]{1,0:T(8,128)(2,1)S(1)} %get-tuple-element.170), channel_id=1, source_target_pairs={{1,0},{2,1},{3,2},{5,4},{6,5},{7,6},{9,8},{10,9},{11,10},{13,12},{... | collective-permute-start | bytes 776 | tf_op jit(solution)/shard_map/while/body/eval_jaxpr/ppermute | solution.py:19
  198.7 6.4 %collective-permute-start.1 = (bf16[128,1]{1,0:T(8,128)(2,1)S(1)}, bf16[128,1]{1,0:T(8,128)(2,1)S(1)}, u32[]{:S(2)}, u32[]{:S(2)}) collective-permute-start(bf16[128,1]{1,0:T(8,128)(2,1)S(1)} %get-tuple-element.171), channel_id=1, source_target_pairs={{0,1},{1,2},{2,3},{4,5},{5,6},{6,7},{8,9},{9,10},{10,11},{12,13},{... | collective-permute-start | bytes 776 | tf_op jit(solution)/shard_map/while/body/eval_jaxpr/ppermute | solution.py:16
  208.2 14.3 %all-to-all-start = ((bf16[64,4,128]{2,1,0:T(4,128)(2,1)}), bf16[64,4,128]{2,1,0:T(4,128)(2,1)S(1)}, u32[]{:S(2)}, u32[]{:S(2)}) async-start(bf16[64,4,128]{2,1,0:T(4,128)(2,1)} %broadcast_select_fusion.2), calls=%async_computation | async-start | bytes 131072 | tf_op jit(solution)/shard_map/while/body/eval_jaxpr/all_to_all | solution.py:65
  222.6 229.2 %copy-start = (f32[128,128]{1,0:T(8,128)}, f32[128,128]{1,0:T(8,128)S(1)}, u32[]{:S(2)}) copy-start(f32[128,128]{1,0:T(8,128)S(1)} %get-tuple-element.81) | copy-start | bytes 196612
  222.6 6.0 %copy-start.1 = (s32[1,128,2]{1,2,0:T(2,128)S(1)}, s32[1,128,2]{1,2,0:T(2,128)}, u32[]{:S(2)}) copy-start(s32[1,128,2]{1,2,0:T(2,128)} %param.18) | copy-start | bytes 3076
  230.1 220.4 %all-reduce.6.cloned.1.call-start = ((), (), s32[]{:S(2)}) async-start(), calls=%async_computation.2 | async-start | bytes 262144 | tf_op jit(solution)/shard_map/psum | solution.py:88
Sparse Core Ops, SparseCore 0:
  230.2 43.9 all-reduce.3
  278.0 172.4 all-reduce.5
